TPU v7x, 32 devices: a whole 2x2x4 slice. The times are simulated.
32 devices in a mesh: fsdp: 4 (over z), tensor: 2 (over core), pool: 4 (over y, x).
Axes of the slice: x: 2, y: 2, z: 4, core: 2. Of those that a mesh axis runs over, the one named last changes fastest.
Arguments:
- hidden: bfloat16 [8192, 5120], P(('fsdp', 'pool'), 'tensor'), may hold values from -6 to 6
- queries: bfloat16 [8192, 5120], P(('fsdp', 'pool'), 'tensor'), may hold values from -200 to 200
- cotangent: bfloat16 [8192, 5120], P(('fsdp', 'pool'), 'tensor'), may hold values from -6 to 6
- segment: int32 [16, 512], P(('fsdp', 'pool')), may hold values from 0 to 15, never falling along the last dimension, each value on 1 to 384 neighbouring positions
- clip_mask: int32 [8192], P(('fsdp', 'pool')), may hold values 0 or 1
- rewards: float32 [256], P(('fsdp', 'pool')), may hold values from 0 to 1
- seq_order: int32 [256], P(('fsdp', 'pool')), may hold values from 0 to 255, each once
- kv_weight: float32 [5120, 2, 1024], P('fsdp', None, 'tensor'), may hold values from -0.078125 to 0.078125
- moment_one: float32 [5120, 2, 1024], P('fsdp', None, 'tensor'), may hold values from -60 to 60
- moment_two: float32 [5120, 2, 1024], P('fsdp', None, 'tensor'), may hold values from 1 to 10000
- dec_hidden: bfloat16 [128, 4, 5120], P(('fsdp', 'pool')), may hold values from -6 to 6
- dec_queries: bfloat16 [128, 4, 5120], P(('fsdp', 'pool'), None, 'tensor'), may hold values from -200 to 200
- kv_cache: bfloat16 [128, 256, 2, 1024], P(('fsdp', 'pool'), None, None, 'tensor'), may hold values from -6 to 6
- cache_len: int32 [128], P(('fsdp', 'pool')), may hold values from 1 to 256
Outputs:
- new_weight: float32 [5120, 2, 1024], P('fsdp', None, 'tensor')
- new_moment_one: float32 [5120, 2, 1024], P('fsdp', None, 'tensor')
- new_moment_two: float32 [5120, 2, 1024], P('fsdp', None, 'tensor')
- dec_out: bfloat16 [128, 4, 5120], P(('fsdp', 'pool'), None, 'tensor')
Inputs may be any that keep to these rules, and one draw needn't show every extreme that they name: `segment`: each row never falls; every sequence number of a row has 1 to 384 tokens. `seq_order`: each place once.
All inputs are finite; a program needn't handle non-finite values. No bound on the sum of `clip_mask` on one device may be relied on, other than what follows from the above.
Results may differ from a plain program's by a relative error of at most 0.014.
The roundings to bfloat16 on the way count: a program that leaves them out, or rounds other values in their place, can miss the bound.
Values may be sent and summed in bfloat16 or wider, within the bound.
No kernel may reach another device: no remote copies, remote signals or barrier semaphores. Data moves between devices by JAX's collectives and lax.ppermute only.
A program may use at most 128 MiB of HBM per device.

v0:
```python
import math
import jax
import jax.numpy as jnp
from jax import lax
from jax.sharding import PartitionSpec as P

D = 5120
QH = 40
KVH = 8
HD = 128
GROUP = 16
beta_one = 0.9
beta_two = 0.999
learn_rate = 0.001
weight_decay = 0.1
adam_epsilon = 1e-08
adam_step = 10.0
variance_floor = 0.04
masked_score = -1e30


def learner_grads(keys_values, queries, cotangent, segment, coefficient):
    block_rows = queries.shape[0]
    head_size = queries.shape[3]
    score_scale = 1.0 / math.sqrt(head_size)
    key_rows = keys_values[:, 0]
    value_rows = keys_values[:, 1]
    scores = (
        jnp.einsum("thrd,uhd->hrtu", queries, key_rows, preferred_element_type=jnp.float32)
        * score_scale
    )
    places = jnp.arange(block_rows)
    allowed = (segment[:, None] == segment[None, :]) & (places[None, :] <= places[:, None])
    scores = jnp.where(allowed, scores, masked_score)
    row_max = jnp.max(scores, axis=-1, keepdims=True)
    weights = jnp.exp(scores - row_max)
    attention = weights / jnp.sum(weights, axis=-1, keepdims=True)
    attention_low = attention.astype(jnp.bfloat16)
    upstream = (coefficient[:, None, None, None] * cotangent.astype(jnp.float32)).astype(
        jnp.bfloat16
    )
    grad_prob = jnp.einsum(
        "thrd,uhd->hrtu", upstream, value_rows, preferred_element_type=jnp.float32
    )
    row_inner = jnp.sum(attention * grad_prob, axis=-1, keepdims=True)
    grad_score = (attention * (grad_prob - row_inner) * score_scale).astype(jnp.bfloat16)
    grad_values = jnp.einsum(
        "hrtu,thrd->uhd", attention_low, upstream, preferred_element_type=jnp.float32
    )
    grad_keys = jnp.einsum(
        "hrtu,thrd->uhd", grad_score, queries, preferred_element_type=jnp.float32
    )
    return jnp.stack([grad_keys, grad_values], axis=1).astype(jnp.bfloat16)


def decode_attend(queries, cache, fresh, lengths):
    head_size = queries.shape[4]
    steps_here = queries.shape[1]
    capacity = cache.shape[1]
    score_scale = 1.0 / math.sqrt(head_size)
    cached = (
        jnp.einsum("bshqd,blhd->bshql", queries, cache[:, :, 0], preferred_element_type=jnp.float32)
        * score_scale
    )
    recent = (
        jnp.einsum("bshqd,bjhd->bshqj", queries, fresh[:, :, 0], preferred_element_type=jnp.float32)
        * score_scale
    )
    live = jnp.arange(capacity)[None, :] < lengths[:, None]
    cached = jnp.where(live[:, None, None, None, :], cached, masked_score)
    before = jnp.arange(steps_here)[None, :] <= jnp.arange(steps_here)[:, None]
    recent = jnp.where(before[None, :, None, None, :], recent, masked_score)
    row_max = jnp.maximum(
        jnp.max(cached, axis=-1, keepdims=True), jnp.max(recent, axis=-1, keepdims=True)
    )
    cached_exp = jnp.exp(cached - row_max)
    recent_exp = jnp.exp(recent - row_max)
    total = jnp.sum(cached_exp, axis=-1, keepdims=True) + jnp.sum(
        recent_exp, axis=-1, keepdims=True
    )
    cached_low = (cached_exp / total).astype(jnp.bfloat16)
    recent_low = (recent_exp / total).astype(jnp.bfloat16)
    output = jnp.einsum(
        "bshql,blhd->bshqd", cached_low, cache[:, :, 1], preferred_element_type=jnp.float32
    )
    output = output + jnp.einsum(
        "bshqj,bjhd->bshqd", recent_low, fresh[:, :, 1], preferred_element_type=jnp.float32
    )
    return output.astype(jnp.bfloat16).reshape(queries.shape[0], steps_here, -1)


def body(
    hidden,
    queries,
    cotangent,
    segment,
    clip_mask,
    rewards,
    seq_order,
    kv_weight,
    moment_one,
    moment_two,
    dec_hidden,
    dec_queries,
    kv_cache,
    cache_len,
):
    block_rows = hidden.shape[0]
    kv_width = kv_weight.shape[2]
    heads_here = kv_width // HD
    head_ratio = QH // KVH
    weight_low = kv_weight.astype(jnp.bfloat16)
    weight_full = lax.all_gather(weight_low, "fsdp", axis=0, tiled=True)
    tokens_full = lax.all_gather(hidden, "tensor", axis=1, tiled=True)
    projected = jnp.dot(
        tokens_full, weight_full.reshape(D, 2 * kv_width), preferred_element_type=jnp.float32
    )
    keys_values = projected.astype(jnp.bfloat16).reshape(block_rows, 2, heads_here, HD)
    shards = lax.axis_size("fsdp") * lax.axis_size("pool")
    groups_total = rewards.shape[0] * shards // GROUP
    group_of = seq_order // GROUP
    onehot = (group_of[:, None] == jnp.arange(groups_total, dtype=jnp.int32)[None, :]).astype(
        jnp.float32
    )
    stats = jnp.stack([rewards, rewards * rewards], axis=1)
    partial_sums = jnp.sum(onehot[:, :, None] * stats[:, None, :], axis=0)
    sums = lax.psum(partial_sums, ("fsdp", "pool"))
    mean = sums[:, 0] / GROUP
    spread = sums[:, 1] / GROUP - mean * mean
    denom = jnp.sqrt(jnp.maximum(spread, variance_floor))
    advantage = (rewards - jnp.sum(onehot * mean[None, :], axis=1)) / jnp.sum(
        onehot * denom[None, :], axis=1
    )
    local_seg = segment[0]
    member = (local_seg[:, None] == jnp.arange(rewards.shape[0], dtype=jnp.int32)[None, :]).astype(
        jnp.float32
    )
    coefficient = jnp.sum(member * advantage[None, :], axis=1) * clip_mask.astype(jnp.float32)
    query_rows = queries.reshape(block_rows, heads_here, head_ratio, HD)
    cot_rows = cotangent.reshape(block_rows, heads_here, head_ratio, HD)
    grad_kv = learner_grads(keys_values, query_rows, cot_rows, local_seg, coefficient).reshape(
        block_rows, 2 * kv_width
    )
    partial_value = jnp.einsum(
        "tc,tk->ck", tokens_full, grad_kv, preferred_element_type=jnp.float32
    )
    shard_grad = lax.psum_scatter(
        partial_value.reshape(kv_weight.shape[0] * lax.axis_size("fsdp"), 2, kv_width).astype(
            jnp.bfloat16
        ),
        "fsdp",
        scatter_dimension=0,
        tiled=True,
    ).astype(jnp.float32)
    grad = lax.psum(shard_grad, "pool")
    new_moment_one = beta_one * moment_one + (1.0 - beta_one) * grad
    new_moment_two = beta_two * moment_two + (1.0 - beta_two) * grad * grad
    first_hat = new_moment_one / (1.0 - beta_one**adam_step)
    second_hat = new_moment_two / (1.0 - beta_two**adam_step)
    new_weight = kv_weight - learn_rate * (
        first_hat / (jnp.sqrt(second_hat) + adam_epsilon) + weight_decay * kv_weight
    )
    dec_rows = dec_hidden.shape[0]
    steps_here = dec_hidden.shape[1]
    capacity = kv_cache.shape[1]
    rollout_low = new_weight.astype(jnp.bfloat16)
    columns = lax.all_to_all(dec_hidden, "fsdp", split_axis=2, concat_axis=0, tiled=True)
    piece_width = columns.shape[2]
    rollout_flat = rollout_low.reshape(piece_width, 2 * kv_width)
    product = jnp.dot(
        columns.reshape(dec_rows * lax.axis_size("fsdp") * steps_here, piece_width),
        rollout_flat,
        preferred_element_type=jnp.float32,
    )
    fresh = lax.psum_scatter(
        product.reshape(dec_rows * lax.axis_size("fsdp"), steps_here, 2 * kv_width),
        "fsdp",
        scatter_dimension=0,
        tiled=True,
    )
    fresh_low = fresh.astype(jnp.bfloat16).reshape(dec_rows, steps_here, 2, heads_here, HD)
    cache = kv_cache.reshape(dec_rows, capacity, 2, heads_here, HD)
    query_dec = dec_queries.reshape(dec_rows, steps_here, heads_here, head_ratio, HD)
    dec_out = decode_attend(query_dec, cache, fresh_low, cache_len)
    return (new_weight, new_moment_one, new_moment_two, dec_out)


def solution(mesh):
    return jax.shard_map(
        body,
        mesh=mesh,
        in_specs=(
            P(("fsdp", "pool"), "tensor"),
            P(("fsdp", "pool"), "tensor"),
            P(("fsdp", "pool"), "tensor"),
            P(("fsdp", "pool"), None),
            P(("fsdp", "pool")),
            P(("fsdp", "pool")),
            P(("fsdp", "pool")),
            P("fsdp", None, "tensor"),
            P("fsdp", None, "tensor"),
            P("fsdp", None, "tensor"),
            P(("fsdp", "pool"), None, None),
            P(("fsdp", "pool"), None, "tensor"),
            P(("fsdp", "pool"), None, None, "tensor"),
            P(("fsdp", "pool")),
        ),
        out_specs=(
            P("fsdp", None, "tensor"),
            P("fsdp", None, "tensor"),
            P("fsdp", None, "tensor"),
            P(("fsdp", "pool"), None, "tensor"),
        ),
        check_vma=False,
    )
```

profile of v0, /device:TPU:0, one launch (start us, length us, event | category | flops | bytes accessed | tf_op | source)
XLA Modules:
  0.0 871.9 jit_solution(16252023753719787070)
XLA Ops:
  7.2 6.2 convert_element_type.64
  13.5 0.7 all-gather.3.cloned.1.call-update
  14.3 3.0 copy.102
  17.3 4.4 copy.99
  21.8 0.1 multiply_reduce_fusion
  21.9 45.7 %psum.14 = f32[16,2]{0,1:T(2,128)S(1)} all-reduce(f32[16,2]{0,1:T(2,128)S(1)} %multiply_reduce_fusion), channel_id=1, replica_groups=mesh['fsdp'=4,'tensor'=2,'pool'=4] {'fsdp','pool'}, use_global_device_ids=true, to_apply=%region_3.4 | all-reduce | flops 32 | bytes 256 | tf_op jit(solution)/shard_map/psum | solution.py:127
  67.6 0.2 select_reduce_fusion.2
  67.8 0.1 select_reduce_fusion
  67.9 0.2 fusion.56
  68.1 132.7 %all-gather.5.cloned.1.call-done = bf16[5120,2,512]{2,1,0:T(2,128)(2,1)} async-done(((bf16[1280,2,512]{2,1,0:T(2,128)(2,1)}), bf16[5120,2,512]{2,1,0:T(2,128)(2,1)}) %all-gather.5.cloned.1.call-update) | async-done | bytes 10485776 | tf_op jit(solution)/shard_map/all_gather | solution.py:113
  200.8 12.6 %copy.142 = bf16[640,8,2,512]{3,1,2,0:T(8,128)(2,1)} copy(bf16[640,8,2,512]{3,2,1,0:T(2,128)(2,1)} %bitcast.179) | data formatting | bytes 20971520
  213.4 2.4 all-gather.3.cloned.1.call-done
  215.8 10.6 %convolution_convert_fusion.1 = bf16[512,1024]{1,0:T(8,128)(2,1)} fusion(bf16[512,5120]{1,0:T(8,128)(2,1)} %all-gather.3.cloned.1.call-done, bf16[5120,1024]{1,0:T(8,128)(2,1)} %bitcast.180), kind=kOutput, calls=%fused_computation.33 | convolution fusion | flops 5369233408 | bytes 16777216 | tf_op jit(solution)/shard_map/dot_general | solution.py:115
  226.4 2.6 reshape.138
  229.0 1.6 fusion.75
  230.6 8.5 fusion.18
  239.0 13.0 %fusion.77 = (f32[4,5,512]{2,1,0:T(8,128)S(1)}, f32[4,5,512,512]{2,3,1,0:T(8,128)}) fusion(pred[512,512]{0,1:T(8,128)(4,1)S(1)} %fusion.56, bf16[512,4,5,128]{0,3,2,1:T(8,128)(2,1)} %bitcast.187, bf16[512,1,4,128]{3,2,1,0:T(4,128)(2,1)S(1)} %get-tuple-element.27), kind=kOutput, calls=%fused_computation.99 | convolution fusion | flops 1363149312 | bytes 24420352 | tf_op jit(solution)/shard_map/sub | solution.py:36
  252.1 8.9 %fusion.43 = bf16[512,1,4,128]{0,3,2,1:T(8,128)(2,1)S(1)} fusion(bf16[512,4,5,128]{0,3,2,1:T(8,128)(2,1)S(1)} %bitcast.184, f32[512]{0:T(512)S(1)} %convert_multiply_fusion.1, f32[4,5,512,512]{2,3,1,0:T(8,128)} %get-tuple-element.31, f32[4,5,512]{2,1,0:T(8,128)S(1)} %get-tuple-element.30), kind=kOutput, calls=%fused_computation.41 | convolution fusion | flops 1356857344 | bytes 24160256 | tf_op jit(solution)/shard_map/hrtu,thrd->uhd/dot_general | solution.py:47
  261.0 27.9 %fusion.48 = bf16[512,1,4,128]{0,3,2,1:T(8,128)(2,1)S(1)} fusion(bf16[512,4,5,128]{0,3,2,1:T(8,128)(2,1)} %bitcast.188, f32[4,512,512,5]{2,1,3,0:T(8,128)} %fusion.18, f32[4,5,512,512]{2,3,1,0:T(8,128)} %get-tuple-element.31, f32[4,5,512]{2,1,0:T(8,128)S(1)} %get-tuple-element.30), kind=kOutput, calls=%fused_computation.42 | convolution fusion | flops 1379150336 | bytes 45129728 | tf_op jit(solution)/shard_map/hrtu,thrd->uhd/dot_general | solution.py:50
  288.9 0.1 pad_maximum_fusion
  289.0 10.8 %convolution_convert_fusion = bf16[1024,5120]{1,0:T(8,128)(2,1)} fusion(bf16[512,1024]{0,1:T(8,128)(2,1)S(1)} %bitcast.190, bf16[512,5120]{1,0:T(8,128)(2,1)} %all-gather.3.cloned.1.call-done), kind=kOutput, calls=%fused_computation.18 | convolution fusion | flops 5373952000 | bytes 16777216 | tf_op jit(solution)/shard_map/tc,tk->ck/dot_general | solution.py:144
  299.8 26.0 %copy.106 = bf16[5120,2,512]{2,1,0:T(2,128)(2,1)} copy(bf16[5120,2,512]{0,2,1:T(8,128)(2,1)} %bitcast.181) | data formatting | bytes 20971520 | tf_op jit(solution)/shard_map/convert_element_type | solution.py:148
  325.9 0.6 copy-done.7
  326.5 0.6 dynamic-slice
  327.8 357.9 %all-reduce.6.cloned.1.call-done = bf16[5120,2,512]{2,1,0:T(2,128)(2,1)} async-done(((bf16[5120,2,512]{2,1,0:T(2,128)(2,1)}), bf16[5120,2,512]{2,1,0:T(2,128)(2,1)}) %all-reduce.6.cloned.1.call-update) | async-done | bytes 10485776
  685.7 6.0 dynamic-slice_convert_fusion
  691.8 5.0 copy.111
  696.7 6.9 reshape.159
  703.6 12.9 %all_to_all.15 = bf16[4,2,20480]{2,1,0:T(2,128)(2,1)S(1)} all-to-all(bf16[4,2,20480]{2,1,0:T(2,128)(2,1)S(1)} %reshape.159), channel_id=1, replica_groups=mesh['fsdp'=4,'tensor'=2,'pool'=4] {'fsdp'}, dimensions={0} | all-to-all | bytes 655360 | tf_op jit(solution)/shard_map/all_to_all | solution.py:167
  716.6 7.2 reshape.160
  723.8 6.7 copy.112
  730.6 81.1 %all-reduce.4.cloned.1.call-done = f32[1280,2,512]{2,1,0:T(2,128)} async-done(((f32[1280,2,512]{2,1,0:T(2,128)}), f32[1280,2,512]{2,1,0:T(2,128)}) %all-reduce.4.cloned.1.call-update) | async-done | bytes 5242896 | tf_op jit(solution)/shard_map/psum | solution.py:155
  811.7 22.5 %fusion.73 = (bf16[1280,2,512]{2,1,0:T(2,128)(2,1)S(1)}, f32[1280,2,512]{2,1,0:T(2,128)}, f32[1280,2,512]{2,1,0:T(2,128)}, f32[1280,2,512]{2,1,0:T(2,128)}) fusion(f32[1280,2,512]{2,1,0:T(2,128)} %param.21, f32[1280,2,512]{2,1,0:T(2,128)} %all-reduce.4.cloned.1.call-done, f32[1280,2,512]{2,1,0:T(2,128)} %param.22, f32[1280,2,512]{2,1,0:T(2,128)} %param.23), kind=kLoop, calls=%fused_computation.96 | loop fusion | flops 20971520 | bytes 39321600 | tf_op jit(solution)/shard_map/convert_element_type | solution.py:166
  834.2 0.7 copy.143
  834.9 0.5 convolution_bitcast_fusion.1
  835.4 0.1 reshape.144
  835.6 1.1 copy.113
  836.7 0.2 reshape.158
  836.9 11.1 %copy.107 = bf16[8,256,2,512]{1,3,2,0:T(8,128)(2,1)} copy(bf16[8,256,2,512]{3,2,1,0:T(2,128)(2,1)} %param.26) | data formatting | bytes 8388608 | tf_op args[12]
  848.1 2.1 fusion.78
  850.2 8.5 reduce-scatter.2.cloned.1.call-done
  858.7 0.9 convert_element_type.79
  859.7 1.3 fusion.79
  861.0 0.2 fusion.63
  861.3 0.5 fusion.57
  861.8 2.3 fusion.51
  864.1 0.4 fusion.53
  864.6 0.8 reshape.156
  (40 shorter events, 0.7 us)
Async XLA Ops:
  7.2 193.7 %all-gather.5.cloned.1.call-start = ((), (), s32[]{:S(2)}) async-start(), calls=%async_computation.3 | async-start | bytes 13107200 | tf_op jit(solution)/shard_map/all_gather | solution.py:113
  13.4 202.4 %all-gather.3.cloned.1.call-start = ((), (), s32[]{:S(2)}) async-start(), calls=%async_computation.2 | async-start | bytes 7864320 | tf_op jit(solution)/shard_map/all_gather | solution.py:114
  14.2 7.5 copy-start.4
  14.2 7.5 copy-start.6
  14.2 53.6 %copy-start.2 = (s32[1,512]{1,0:T(1,128)S(1)}, s32[1,512]{1,0:T(1,128)}, u32[]{:S(2)}) copy-start(s32[1,512]{1,0:T(1,128)} %param.17) | copy-start | bytes 6148
  14.2 53.7 %copy-start.3 = (s32[512]{0:T(512)S(1)}, s32[512]{0:T(512)}, u32[]{:S(2)}) copy-start(s32[512]{0:T(512)} %param.18) | copy-start | bytes 6148
  14.2 671.5 %all-reduce.6.cloned.1.call-start = ((), (), s32[]{:S(2)}) async-start(), calls=%async_computation.6 | async-start | bytes 20971520
  325.9 0.7 copy-start.7
  325.9 485.8 %all-reduce.4.cloned.1.call-start = ((), (), s32[]{:S(2)}) async-start(), calls=%async_computation.4 | async-start | bytes 10485760 | tf_op jit(solution)/shard_map/psum | solution.py:155
  327.8 364.0 %copy-start = (bf16[8,4,5120]{2,1,0:T(4,128)(2,1)S(1)}, bf16[8,4,5120]{2,1,0:T(4,128)(2,1)}, u32[]{:S(2)}) copy-start(bf16[8,4,5120]{2,1,0:T(4,128)(2,1)} %param.24) | copy-start | bytes 983044
  691.7 167.0 %reduce-scatter.2.cloned.1.call-start = ((), (), s32[]{:S(2)}) async-start(), calls=%async_computation.5 | async-start | bytes 655360 | tf_op jit(solution)/shard_map/reduce_scatter | solution.py:175
  834.2 2.5 copy-start.1
  835.6 12.4 %copy-start.5 = (s32[8]{0:T(128)S(1)}, s32[8]{0:T(128)}, u32[]{:S(2)}) copy-start(s32[8]{0:T(128)} %param.27) | copy-start | bytes 100
Sparse Core Ops, SparseCore 0:
  13.5 187.2 all-gather.4
  202.4 13.4 all-gather.2
  326.0 359.6 all-reduce.5
  691.8 119.8 all-reduce.3
  836.9 21.8 reduce-scatter.1
where the time goes:
time: 874 us; the launch traced here: 872 us
  waiting for transfers between devices  583 us (67%)
  local copies, waits for them, and re-layouts  91.3 us (10%)
  matrix products  86.4 us (10%)
  blocking collectives  58.7 us (7%)
  other arithmetic  37.2 us (4%)
  between operations  14.7 us (2%)
    unnamed x6, waiting for transfers between devices  359 us
    all_gather x1, waiting for transfers between devices, body(): weight_full = lax.all_gather(weight_low, 'fsdp', axis=0, tiled=True)  133 us
    psum x1, waiting for transfers between devices, body(): grad = lax.psum(shard_grad, 'pool')  81.1 us
    unnamed x27, local copies, waits for them, and re-layouts  52.8 us
    psum x1, blocking collectives, body(): sums = lax.psum(partial_sums, ('fsdp', 'pool'))  45.7 us
    dot_general x1, matrix products, learner_grads(): jnp.einsum('hrtu,thrd->uhd', grad_score, queries, preferred_element_type=...  27.9 us
    convert_element_type x1, local copies, waits for them, and re-layouts, body(): partial_value.reshape(kv_weight.shape[0] * lax.axis_size('fsdp'), 2, kv_w...  26 us
    convert_element_type x1, other arithmetic, body(): rollout_low = new_weight.astype(jnp.bfloat16)  22.5 us
  transfers between devices with their start and end apart: 5, of which 5 were waited for; matrix products, arithmetic and copies ran while one was open for 7% of the time, Pallas kernels for 0%

commit v1 on v0

--- a/solution.py
+++ b/solution.py
@@ -17,6 +17,10 @@
 adam_step = 10.0
 variance_floor = 0.04
 masked_score = -1e30
+
+
+def figure_build(chunk, axis_key):
+    return jnp.sum(jax.lax.all_gather(chunk, axis_key), axis=0)
 
 
 def learner_grads(keys_values, queries, cotangent, segment, coefficient):
@@ -152,7 +156,7 @@
         scatter_dimension=0,
         tiled=True,
     ).astype(jnp.float32)
-    grad = lax.psum(shard_grad, "pool")
+    grad = figure_build(shard_grad, "pool")
     new_moment_one = beta_one * moment_one + (1.0 - beta_one) * grad
     new_moment_two = beta_two * moment_two + (1.0 - beta_two) * grad * grad
     first_hat = new_moment_one / (1.0 - beta_one**adam_step)

time: 874 us -> 794 us (0.908)
  waiting for transfers between devices: 583 us -> 451 us
  local copies, waits for them, and re-layouts: 91.3 us -> 142 us
  blocking collectives: 58.7 us -> 45.7 us
  other arithmetic: 37.2 us -> 46.1 us
    unnamed x6 -> x5, waiting for transfers between devices: 359 us -> 0.76 us
    reduce_scatter x0 -> x1, waiting for transfers between devices: none -> 179 us  [body(): lax.psum_scatter(partial_value.reshape(kv_weight.shape[0] * lax.axis_size...]
    all_gather x0 -> x1, waiting for transfers between devices: none -> 136 us  [figure_build(): return jnp.sum(jax.lax.all_gather(chunk, axis_key), axis=0)]
    psum x1 -> x0, waiting for transfers between devices: 81.1 us -> none  [body(): grad = lax.psum(shard_grad, 'pool')]
    unnamed x27 -> x29, local copies, waits for them, and re-layouts: 52.8 us -> 104 us
    convert_element_type x1 -> x0, local copies, waits for them, and re-layouts: 26 us -> none  [body(): partial_value.reshape(kv_weight.shape[0] * lax.axis_size('fsdp'), 2, kv_w...]
    all_gather x0 -> x1, local copies, waits for them, and re-layouts: none -> 25.3 us  [figure_build(): return jnp.sum(jax.lax.all_gather(chunk, axis_key), axis=0)]
    reduce_sum x0 -> x1, other arithmetic: none -> 18.5 us  [figure_build(): return jnp.sum(jax.lax.all_gather(chunk, axis_key), axis=0)]
  transfers between devices with their start and end apart: 5 -> 6, of which waited for: 5 -> 4; matrix products, arithmetic and copies ran while one was open for 7% -> 14% of each run, Pallas kernels for 0% -> 0%
where the time goes in v1:
time: 794 us; the launch traced here: 791 us
  waiting for transfers between devices  451 us (57%)
  local copies, waits for them, and re-layouts  142 us (18%)
  matrix products  86.9 us (11%)
  other arithmetic  46.1 us (6%)
  blocking collectives  45.7 us (6%)
  between operations  14 us (2%)
    reduce_scatter x1, waiting for transfers between devices, body(): lax.psum_scatter(partial_value.reshape(kv_weight.shape[0] * lax.axis_size...  179 us
    all_gather x1, waiting for transfers between devices, figure_build(): return jnp.sum(jax.lax.all_gather(chunk, axis_key), axis=0)  136 us
    all_gather x1, waiting for transfers between devices, body(): weight_full = lax.all_gather(weight_low, 'fsdp', axis=0, tiled=True)  133 us
    unnamed x29, local copies, waits for them, and re-layouts  104 us
    psum x1, blocking collectives, body(): sums = lax.psum(partial_sums, ('fsdp', 'pool'))  45.7 us
    dot_general x1, matrix products, learner_grads(): jnp.einsum('hrtu,thrd->uhd', grad_score, queries, preferred_element_type=...  27.9 us
    all_gather x1, local copies, waits for them, and re-layouts, figure_build(): return jnp.sum(jax.lax.all_gather(chunk, axis_key), axis=0)  25.3 us
    reduce_sum x1, other arithmetic, figure_build(): return jnp.sum(jax.lax.all_gather(chunk, axis_key), axis=0)  18.5 us
  transfers between devices with their start and end apart: 6, of which 4 were waited for; matrix products, arithmetic and copies ran while one was open for 14% of the time, Pallas kernels for 0%

profile of v1, /device:TPU:0, one launch (start us, length us, event | category | flops | bytes accessed | tf_op | source)
XLA Modules:
  0.0 791.1 jit_solution(3759210770665864972)
XLA Ops:
  7.2 6.2 convert_element_type.62
  13.5 0.7 all-gather.5.cloned.1.call-update
  14.3 3.0 copy.113
  17.3 4.4 copy.110
  21.9 45.7 %psum.7 = f32[16,2]{0,1:T(2,128)S(1)} all-reduce(f32[16,2]{0,1:T(2,128)S(1)} %multiply_reduce_fusion), channel_id=1, replica_groups=mesh['fsdp'=4,'tensor'=2,'pool'=4] {'fsdp','pool'}, use_global_device_ids=true, to_apply=%region_3.4 | all-reduce | flops 32 | bytes 256 | tf_op jit(solution)/shard_map/psum | solution.py:131
  67.6 0.2 select_reduce_fusion.2
  67.9 0.2 fusion.56
  68.1 132.7 %all-gather.7.cloned.1.call-done = bf16[5120,2,512]{2,1,0:T(2,128)(2,1)} async-done(((bf16[1280,2,512]{2,1,0:T(2,128)(2,1)}), bf16[5120,2,512]{2,1,0:T(2,128)(2,1)}) %all-gather.7.cloned.1.call-update) | async-done | bytes 10485776 | tf_op jit(solution)/shard_map/all_gather | solution.py:117
  200.8 12.6 %copy.158 = bf16[640,8,2,512]{3,1,2,0:T(8,128)(2,1)} copy(bf16[640,8,2,512]{3,2,1,0:T(2,128)(2,1)} %bitcast.179) | data formatting | bytes 20971520
  213.4 2.4 all-gather.5.cloned.1.call-done
  215.8 10.6 %convolution_convert_fusion.1 = bf16[512,1024]{1,0:T(8,128)(2,1)} fusion(bf16[512,5120]{1,0:T(8,128)(2,1)} %all-gather.5.cloned.1.call-done, bf16[5120,1024]{1,0:T(8,128)(2,1)} %bitcast.181), kind=kOutput, calls=%fused_computation.32 | convolution fusion | flops 5369233408 | bytes 16777216 | tf_op jit(solution)/shard_map/dot_general | solution.py:119
  226.4 2.6 reshape.138
  229.0 1.6 fusion.75
  230.6 8.5 %fusion.18 = f32[4,512,512,5]{2,1,3,0:T(8,128)} fusion(bf16[512,4,5,128]{0,3,2,1:T(8,128)(2,1)S(1)} %bitcast.182, f32[512]{0:T(512)S(1)} %convert_multiply_fusion.1, bf16[512,1,4,128]{3,2,1,0:T(4,128)(2,1)S(1)} %get-tuple-element.26), kind=kOutput, calls=%fused_computation.26 | convolution fusion | flops 1346109440 | bytes 24119296 | tf_op jit(solution)/shard_map/thrd,uhd->hrtu/dot_general | solution.py:46
  239.0 13.0 %fusion.77 = (f32[4,5,512]{2,1,0:T(8,128)S(1)}, f32[4,5,512,512]{2,3,1,0:T(8,128)}) fusion(pred[512,512]{0,1:T(8,128)(4,1)S(1)} %fusion.56, bf16[512,4,5,128]{0,3,2,1:T(8,128)(2,1)} %bitcast.186, bf16[512,1,4,128]{3,2,1,0:T(4,128)(2,1)S(1)} %get-tuple-element.27), kind=kOutput, calls=%fused_computation.98 | convolution fusion | flops 1363149312 | bytes 24420352 | tf_op jit(solution)/shard_map/sub | solution.py:40
  252.1 8.9 %fusion.43 = bf16[512,1,4,128]{0,3,2,1:T(8,128)(2,1)S(1)} fusion(bf16[512,4,5,128]{0,3,2,1:T(8,128)(2,1)S(1)} %bitcast.183, f32[512]{0:T(512)S(1)} %convert_multiply_fusion.1, f32[4,5,512,512]{2,3,1,0:T(8,128)} %get-tuple-element.31, f32[4,5,512]{2,1,0:T(8,128)S(1)} %get-tuple-element.30), kind=kOutput, calls=%fused_computation.40 | convolution fusion | flops 1356857344 | bytes 24160256 | tf_op jit(solution)/shard_map/hrtu,thrd->uhd/dot_general | solution.py:51
  261.0 27.9 %fusion.48 = bf16[512,1,4,128]{0,3,2,1:T(8,128)(2,1)S(1)} fusion(bf16[512,4,5,128]{0,3,2,1:T(8,128)(2,1)} %bitcast.187, f32[4,512,512,5]{2,1,3,0:T(8,128)} %fusion.18, f32[4,5,512,512]{2,3,1,0:T(8,128)} %get-tuple-element.31, f32[4,5,512]{2,1,0:T(8,128)S(1)} %get-tuple-element.30), kind=kOutput, calls=%fused_computation.41 | convolution fusion | flops 1379150336 | bytes 45129728 | tf_op jit(solution)/shard_map/hrtu,thrd->uhd/dot_general | solution.py:54
  289.0 10.8 %convolution_convert_fusion = bf16[1024,5120]{1,0:T(8,128)(2,1)} fusion(bf16[512,1024]{0,1:T(8,128)(2,1)S(1)} %bitcast.189, bf16[512,5120]{1,0:T(8,128)(2,1)} %all-gather.5.cloned.1.call-done), kind=kOutput, calls=%fused_computation.18 | convolution fusion | flops 5373952000 | bytes 16777216 | tf_op jit(solution)/shard_map/tc,tk->ck/dot_general | solution.py:148
  299.9 179.3 %reduce-scatter.3.cloned.1.call-done = bf16[1280,2,512]{0,2,1:T(8,128)(2,1)} async-done(((bf16[5120,2,512]{0,2,1:T(8,128)(2,1)}), bf16[1280,2,512]{0,2,1:T(8,128)(2,1)}) %reduce-scatter.3.cloned.1.call-update) | async-done | bytes 2621456 | tf_op jit(solution)/shard_map/reduce_scatter | solution.py:151
  479.2 4.5 all_gather.20
  483.8 5.0 copy.124
  488.7 7.9 %reshape.160 = bf16[4,2,20480]{2,1,0:T(2,128)(2,1)} reshape(bf16[5120,4,8]{2,1,0:T(4,128)(2,1)} %bitcast.177) | data formatting | bytes 655360
  496.7 4.7 all-to-all-start
  501.4 8.8 %copy.119 = f32[1280,2,512]{0,2,1:T(8,128)} copy(f32[1280,2,512]{2,1,0:T(2,128)} %param.21) | data formatting | bytes 10485760 | tf_op args[7]
  510.2 8.7 %copy.108 = f32[1280,2,512]{0,2,1:T(8,128)} copy(f32[1280,2,512]{2,1,0:T(2,128)} %param.22) | data formatting | bytes 10485760 | tf_op args[8]
  518.8 8.9 %copy.117 = f32[1280,2,512]{0,2,1:T(8,128)} copy(f32[1280,2,512]{2,1,0:T(2,128)} %param.23) | data formatting | bytes 10485760 | tf_op args[9]
  527.7 7.3 reshape.161
  535.0 6.7 copy.125
  541.7 136.3 %all-gather.9.cloned.1.call-done = f32[5120,2,512]{0,2,1:T(8,128)} async-done(((f32[1280,2,512]{0,2,1:T(8,128)}), f32[5120,2,512]{0,2,1:T(8,128)}) %all-gather.9.cloned.1.call-update) | async-done | bytes 20971536 | tf_op jit(solution)/shard_map/all_gather | solution.py:23
  678.0 25.3 %reshape.149 = f32[4,1280,2,512]{1,0,3,2:T(4,128)} reshape(f32[5120,2,512]{0,2,1:T(8,128)} %all-gather.9.cloned.1.call-done) | data formatting | bytes 41943040 | tf_op jit(solution)/shard_map/all_gather | solution.py:23
  703.3 18.5 %reduce_sum.87 = f32[1280,2,512]{0,2,1:T(8,128)} reduce(f32[4,1280,2,512]{1,0,3,2:T(4,128)} %reshape.149, f32[]{:T(128)} %constant.37.clone.1), dimensions={0}, to_apply=%region_9.10 | reduce | flops 3932160 | bytes 26214404 | tf_op jit(solution)/shard_map/reduce_sum | solution.py:23
  721.8 14.3 %fusion.73 = (bf16[1280,2,512]{0,2,1:T(8,128)(2,1)S(1)}, f32[1280,2,512]{0,2,1:T(8,128)}, f32[1280,2,512]{0,2,1:T(8,128)}, f32[1280,2,512]{0,2,1:T(8,128)}) fusion(f32[1280,2,512]{0,2,1:T(8,128)} %copy.119, f32[1280,2,512]{0,2,1:T(8,128)} %reduce_sum.87, f32[1280,2,512]{0,2,1:T(8,128)} %copy.108, f32[1280,2,512]{0,2,1:T(8,128)} %copy.117), kind=kLoop, calls=%fused_computation.95 | loop fusion | flops 20971520 | bytes 39321600 | tf_op jit(solution)/shard_map/convert_element_type | solution.py:170
  736.1 1.0 convolution_bitcast_fusion.1
  737.1 0.1 reshape.144
  737.3 1.1 copy.126
  738.4 0.2 reshape.159
  738.6 11.1 %copy.120 = bf16[8,256,2,512]{1,3,2,0:T(8,128)(2,1)} copy(bf16[8,256,2,512]{3,2,1,0:T(2,128)(2,1)} %param.26) | data formatting | bytes 8388608 | tf_op args[12]
  749.8 2.1 fusion.78
  751.9 8.7 %copy.132 = f32[1280,2,512]{2,1,0:T(2,128)} copy(f32[1280,2,512]{0,2,1:T(8,128)} %get-tuple-element.23) | data formatting | bytes 10485760
  760.6 8.7 %copy.133 = f32[1280,2,512]{2,1,0:T(2,128)} copy(f32[1280,2,512]{0,2,1:T(8,128)} %get-tuple-element.24) | data formatting | bytes 10485760
  769.3 8.7 %copy.134 = f32[1280,2,512]{2,1,0:T(2,128)} copy(f32[1280,2,512]{0,2,1:T(8,128)} %get-tuple-element.25) | data formatting | bytes 10485760
  778.0 0.9 convert_element_type.76
  779.0 1.3 fusion.79
  780.3 0.2 fusion.63
  780.6 0.5 fusion.57
  781.1 2.3 fusion.51
  783.4 0.4 fusion.53
  783.8 0.8 reshape.158
  (44 shorter events, 1.0 us)
Async XLA Ops:
  7.2 193.7 %all-gather.7.cloned.1.call-start = ((), (), s32[]{:S(2)}) async-start(), calls=%async_computation.4 | async-start | bytes 13107200 | tf_op jit(solution)/shard_map/all_gather | solution.py:117
  13.4 202.4 %all-gather.5.cloned.1.call-start = ((), (), s32[]{:S(2)}) async-start(), calls=%async_computation.3 | async-start | bytes 7864320 | tf_op jit(solution)/shard_map/all_gather | solution.py:118
  14.2 7.5 copy-start.4
  14.2 7.5 copy-start.6
  14.2 53.6 %copy-start.2 = (s32[1,512]{1,0:T(1,128)S(1)}, s32[1,512]{1,0:T(1,128)}, u32[]{:S(2)}) copy-start(s32[1,512]{1,0:T(1,128)} %param.17) | copy-start | bytes 6148
  14.2 53.7 %copy-start.3 = (s32[512]{0:T(512)S(1)}, s32[512]{0:T(512)}, u32[]{:S(2)}) copy-start(s32[512]{0:T(512)} %param.18) | copy-start | bytes 6148
  14.2 465.0 %reduce-scatter.3.cloned.1.call-start = ((), (), s32[]{:S(2)}) async-start(), calls=%async_computation.5 | async-start | bytes 13107200 | tf_op jit(solution)/shard_map/reduce_scatter | solution.py:151
  299.9 183.9 %copy-start = (bf16[8,4,5120]{2,1,0:T(4,128)(2,1)S(1)}, bf16[8,4,5120]{2,1,0:T(4,128)(2,1)}, u32[]{:S(2)}) copy-start(bf16[8,4,5120]{2,1,0:T(4,128)(2,1)} %param.24) | copy-start | bytes 983044
  299.9 378.1 %all-gather.9.cloned.1.call-start = ((), (), s32[]{:S(2)}) async-start(), calls=%async_computation.7 | async-start | bytes 26214400 | tf_op jit(solution)/shard_map/all_gather | solution.py:23
  496.7 31.1 %all-to-all-start = ((bf16[4,2,20480]{2,1,0:T(2,128)(2,1)}), bf16[4,2,20480]{2,1,0:T(2,128)(2,1)S(1)}, u32[]{:S(2)}, u32[]{:S(2)}) async-start(bf16[4,2,20480]{2,1,0:T(2,128)(2,1)} %reshape.160), calls=%async_computation.1 | async-start | bytes 655360 | tf_op jit(solution)/shard_map/all_to_all | solution.py:171
  501.4 276.6 %reduce-scatter.5.cloned.1.call-start = ((), (), s32[]{:S(2)}) async-start(), calls=%async_computation.6 | async-start | bytes 655360 | tf_op jit(solution)/shard_map/reduce_scatter | solution.py:179
  736.1 2.3 copy-start.1
  737.3 12.4 %copy-start.5 = (s32[8]{0:T(128)S(1)}, s32[8]{0:T(128)}, u32[]{:S(2)}) copy-start(s32[8]{0:T(128)} %param.27) | copy-start | bytes 100
Sparse Core Ops, SparseCore 0:
  13.5 187.2 all-gather.6
  202.4 13.4 all-gather.4
  300.0 179.2 reduce-scatter.2
  483.9 194.0 all-gather.8
  738.5 21.8 reduce-scatter.4
